TPU v7x, 32 devices: a whole 2x2x4 slice. The times are simulated.
32 devices in a mesh: dp: 8 (over z, y), mp: 4 (over x, core).
Axes of the slice: x: 2, y: 2, z: 4, core: 2. Of those that a mesh axis runs over, the one named last changes fastest.
Arguments:
- tokens: bfloat16 [8192, 768], P(('dp', 'mp')), may hold values from -6 to 6
- segment_ids: int32 [8192], P('dp'), may hold values from 0 to 10, as said below
- keep_mask: int32 [88, 2], P('dp'), may hold values 0 or 1
- first_gain: bfloat16 [768], replicated, may hold values from 0.5 to 1.5
- first_shift: bfloat16 [768], replicated, may hold values from -3 to 3
- query_weight: bfloat16 [768, 768], P(None, 'mp'), may hold values from -0.21875 to 0.21875
- query_bias: bfloat16 [768], P('mp'), may hold values from -3 to 3
- key_weight: bfloat16 [768, 768], P(None, 'mp'), may hold values from -0.21875 to 0.21875
- value_weight: bfloat16 [768, 768], P(None, 'mp'), may hold values from -0.21875 to 0.21875
- value_bias: bfloat16 [768], P('mp'), may hold values from -3 to 3
- out_weight: bfloat16 [768, 768], P('mp'), may hold values from -2.5 to 2.5
- out_bias: bfloat16 [768], replicated, may hold values from -2 to 2
- second_gain: bfloat16 [768], replicated, may hold values from 0.5 to 1.5
- second_shift: bfloat16 [768], replicated, may hold values from -3 to 3
- up_weight: bfloat16 [768, 3072], P(None, 'mp'), may hold values from -0.21875 to 0.21875
- up_bias: bfloat16 [3072], P('mp'), may hold values from -3 to 3
- down_weight: bfloat16 [3072, 768], P('mp'), may hold values from -0.109375 to 0.109375
- down_bias: bfloat16 [768], replicated, may hold values from -2 to 2
- cotangent: bfloat16 [8192, 768], P(('dp', 'mp')), may hold values from -6 to 6
Outputs:
- layer_out: bfloat16 [8192, 768], P(('dp', 'mp'))
- input_grad: float32 [8192, 768], P(('dp', 'mp'))
- first_gain_grad: float32 [768], replicated
- first_shift_grad: float32 [768], replicated
- query_weight_grad: float32 [768, 768], P(None, 'mp')
- query_bias_grad: float32 [768], P('mp')
- key_weight_grad: float32 [768, 768], P(None, 'mp')
- value_weight_grad: float32 [768, 768], P(None, 'mp')
- value_bias_grad: float32 [768], P('mp')
- out_weight_grad: float32 [768, 768], P('mp')
- out_bias_grad: float32 [768], replicated
- second_gain_grad: float32 [768], replicated
- second_shift_grad: float32 [768], replicated
- up_weight_grad: float32 [768, 3072], P(None, 'mp')
- up_bias_grad: float32 [3072], P('mp')
- down_weight_grad: float32 [3072, 768], P('mp')
- down_bias_grad: float32 [768], replicated
Inputs may be any that keep to these rules, and one draw needn't show every extreme that they name: `segment_ids`: within each aligned block of 1024 tokens the ids start at 0, never fall and rise by one from image to image; every image but the last of a block has 102, 198 or 578 tokens, the last holds the remaining tokens. In the first block every image but the last has 102 tokens. `keep_mask`: row i of a block of 11 rows belongs to the image with segment id i of the same index of dp.
All inputs are finite; a program needn't handle non-finite values.
Results may differ from a plain program's by a relative error of at most 0.02.
Values may be sent and summed in bfloat16 or wider, within the bound.
No kernel may reach another device: no remote copies, remote signals or barrier semaphores. Data moves between devices by JAX's collectives and lax.ppermute only.
A program may use at most 128 MiB of HBM per device.

v0:
```python
import math
import jax
import jax.numpy as jnp
from jax import lax
from jax.sharding import PartitionSpec as P

HD = 64
eps = 1e-06


def layer_norm(values, scaling, bias_add):
    center = values - jnp.mean(values, axis=-1, keepdims=True)
    spread = jnp.mean(center * center, axis=-1, keepdims=True)
    return center * lax.rsqrt(spread + eps) * scaling + bias_add


def gelu_exact(values):
    return jax.nn.gelu(values, approximate=False)


def per_device(
    tokens,
    segment_ids,
    keep_mask,
    first_gain,
    first_shift,
    query_weight,
    query_bias,
    key_weight,
    value_weight,
    value_bias,
    out_weight,
    out_bias,
    second_gain,
    second_shift,
    up_weight,
    up_bias,
    down_weight,
    down_bias,
    cotangent,
):
    f32 = jnp.float32
    bf16 = jnp.bfloat16
    local_rows = tokens.shape[0]
    row_count = segment_ids.shape[0]
    head_width = query_weight.shape[1]
    head_group = head_width // HD
    score_scale = 1.0 / math.sqrt(HD)
    block_rows = min(512, row_count)
    block_count = row_count // block_rows
    offset = lax.axis_index("mp") * local_rows
    local_ids = lax.dynamic_slice_in_dim(segment_ids, offset, local_rows)
    onehot = (
        local_ids[:, None] == jnp.arange(keep_mask.shape[0], dtype=jnp.int32)[None, :]
    ).astype(f32)
    keep_rows = jnp.dot(onehot, keep_mask.astype(f32), precision=lax.Precision.HIGHEST) / 0.9
    allowed = segment_ids[:, None] == segment_ids[None, :]
    gain_one = first_gain.astype(f32)
    shift_one = first_shift.astype(f32)
    gain_two = second_gain.astype(f32)
    shift_two = second_shift.astype(f32)
    inputs = tokens.astype(f32)
    normed = layer_norm(inputs, gain_one, shift_one).astype(bf16)
    normed_all = lax.all_gather(normed, "mp", axis=0, tiled=True)
    query_rows = (
        jnp.dot(normed_all, query_weight, preferred_element_type=f32) + query_bias.astype(f32)
    ).astype(bf16)
    key_rows = jnp.dot(normed_all, key_weight, preferred_element_type=f32).astype(bf16)
    value_rows = (
        jnp.dot(normed_all, value_weight, preferred_element_type=f32) + value_bias.astype(f32)
    ).astype(bf16)
    key_heads = key_rows.reshape(row_count, head_group, HD)
    value_heads = value_rows.reshape(row_count, head_group, HD)
    context_parts = []
    lse_parts = []
    for number in range(block_count):
        row_start = number * block_rows
        query_block = query_rows[row_start : row_start + block_rows].reshape(
            block_rows, head_group, HD
        )
        scores = (
            jnp.einsum("qhd,khd->hqk", query_block, key_heads, preferred_element_type=f32)
            * score_scale
        )
        scores = jnp.where(allowed[row_start : row_start + block_rows][None], scores, -1e30)
        largest = jnp.max(scores, axis=-1, keepdims=True)
        powers = jnp.exp(scores - largest)
        totals = jnp.sum(powers, axis=-1, keepdims=True)
        weights = (powers / totals).astype(bf16)
        context_block = jnp.einsum("hqk,khd->qhd", weights, value_heads, preferred_element_type=f32)
        context_parts.append(context_block.reshape(block_rows, head_width))
        lse_parts.append(largest + jnp.log(totals))
    context = jnp.concatenate(context_parts, axis=0).astype(bf16)
    attended = lax.psum_scatter(
        jnp.dot(context, out_weight, preferred_element_type=f32).astype(jnp.bfloat16),
        "mp",
        scatter_dimension=0,
        tiled=True,
    ).astype(jnp.float32) + out_bias.astype(f32)
    middle = inputs + keep_rows[:, 0:1] * attended
    normed_two = layer_norm(middle, gain_two, shift_two).astype(bf16)
    normed_two_all = lax.all_gather(normed_two, "mp", axis=0, tiled=True)
    hidden = jnp.dot(normed_two_all, up_weight, preferred_element_type=f32) + up_bias.astype(f32)
    activated = gelu_exact(hidden).astype(bf16)
    mlp_out = lax.psum_scatter(
        jnp.dot(activated, down_weight, preferred_element_type=f32).astype(jnp.bfloat16),
        "mp",
        scatter_dimension=0,
        tiled=True,
    ).astype(jnp.float32) + down_bias.astype(f32)
    layer_out = (middle + keep_rows[:, 1:2] * mlp_out).astype(bf16)
    out_grad = cotangent.astype(f32)
    mlp_grad = out_grad * keep_rows[:, 1:2]
    down_bias_grad = jnp.sum(mlp_grad, axis=0)
    mlp_grad_all = lax.all_gather(mlp_grad.astype(bf16), "mp", axis=0, tiled=True)
    down_weight_grad = jnp.einsum("rf,rd->fd", activated, mlp_grad_all, preferred_element_type=f32)
    act_grad = jnp.einsum("rd,fd->rf", mlp_grad_all, down_weight, preferred_element_type=f32)
    unused_value, gelu_pull = jax.vjp(gelu_exact, hidden)
    hidden_grad = gelu_pull(act_grad)[0].astype(bf16)
    up_bias_grad = jnp.sum(hidden_grad.astype(f32), axis=0)
    up_weight_grad = jnp.einsum(
        "rd,rf->df", normed_two_all, hidden_grad, preferred_element_type=f32
    )
    second_grad = lax.psum_scatter(
        jnp.einsum("rf,df->rd", hidden_grad, up_weight, preferred_element_type=f32).astype(
            jnp.bfloat16
        ),
        "mp",
        scatter_dimension=0,
        tiled=True,
    ).astype(jnp.float32)
    unused_value, norm_pull_two = jax.vjp(layer_norm, middle, gain_two, shift_two)
    middle_part, gain_two_grad, shift_two_grad = norm_pull_two(second_grad)
    middle_grad = out_grad + middle_part
    attn_grad = middle_grad * keep_rows[:, 0:1]
    out_bias_grad = jnp.sum(attn_grad, axis=0)
    attn_grad_all = lax.all_gather(attn_grad.astype(bf16), "mp", axis=0, tiled=True)
    out_weight_grad = jnp.einsum("rc,rd->cd", context, attn_grad_all, preferred_element_type=f32)
    context_grad = jnp.einsum(
        "rd,cd->rc", attn_grad_all, out_weight, preferred_element_type=f32
    ).astype(bf16)
    context_grad_heads = context_grad.reshape(row_count, head_group, HD)
    query_grads = []
    key_grad = jnp.zeros((row_count, head_group, HD), f32)
    value_grad = jnp.zeros((row_count, head_group, HD), f32)
    for number in range(block_count):
        row_start = number * block_rows
        query_block = query_rows[row_start : row_start + block_rows].reshape(
            block_rows, head_group, HD
        )
        scores = (
            jnp.einsum("qhd,khd->hqk", query_block, key_heads, preferred_element_type=f32)
            * score_scale
        )
        scores = jnp.where(allowed[row_start : row_start + block_rows][None], scores, -1e30)
        probs = jnp.exp(scores - lse_parts[number])
        grad_block = context_grad_heads[row_start : row_start + block_rows]
        prob_grad = jnp.einsum("qhd,khd->hqk", grad_block, value_heads, preferred_element_type=f32)
        center = jnp.sum(probs * prob_grad, axis=-1, keepdims=True)
        score_grad = (probs * (prob_grad - center)).astype(bf16)
        query_grads.append(
            jnp.einsum("hqk,khd->qhd", score_grad, key_heads, preferred_element_type=f32)
            * score_scale
        )
        key_grad = (
            key_grad
            + jnp.einsum("hqk,qhd->khd", score_grad, query_block, preferred_element_type=f32)
            * score_scale
        )
        value_grad = value_grad + jnp.einsum(
            "hqk,qhd->khd", probs.astype(bf16), grad_block, preferred_element_type=f32
        )
    query_grad_rows = (
        jnp.concatenate(query_grads, axis=0).reshape(row_count, head_width).astype(bf16)
    )
    key_grad_rows = key_grad.reshape(row_count, head_width).astype(bf16)
    value_grad_rows = value_grad.reshape(row_count, head_width).astype(bf16)
    query_bias_grad = jnp.sum(query_grad_rows.astype(f32), axis=0)
    value_bias_grad = jnp.sum(value_grad_rows.astype(f32), axis=0)
    query_weight_grad = jnp.einsum(
        "rd,rc->dc", normed_all, query_grad_rows, preferred_element_type=f32
    )
    key_weight_grad = jnp.einsum("rd,rc->dc", normed_all, key_grad_rows, preferred_element_type=f32)
    value_weight_grad = jnp.einsum(
        "rd,rc->dc", normed_all, value_grad_rows, preferred_element_type=f32
    )
    total = jnp.einsum("rc,dc->rd", query_grad_rows, query_weight, preferred_element_type=f32)
    total = total + jnp.einsum("rc,dc->rd", key_grad_rows, key_weight, preferred_element_type=f32)
    first_grad = lax.psum_scatter(
        (
            total
            + jnp.einsum("rc,dc->rd", value_grad_rows, value_weight, preferred_element_type=f32)
        ).astype(jnp.bfloat16),
        "mp",
        scatter_dimension=0,
        tiled=True,
    ).astype(jnp.float32)
    unused_value, norm_pull_one = jax.vjp(layer_norm, inputs, gain_one, shift_one)
    input_part, gain_one_grad, shift_one_grad = norm_pull_one(first_grad)
    input_grad = middle_grad + input_part
    (
        query_weight_grad,
        query_bias_grad,
        key_weight_grad,
        value_weight_grad,
        value_bias_grad,
        out_weight_grad,
        up_weight_grad,
        up_bias_grad,
        down_weight_grad,
    ) = lax.psum(
        (
            query_weight_grad,
            query_bias_grad,
            key_weight_grad,
            value_weight_grad,
            value_bias_grad,
            out_weight_grad,
            up_weight_grad,
            up_bias_grad,
            down_weight_grad,
        ),
        "dp",
    )
    gain_one_grad, shift_one_grad, out_bias_grad, gain_two_grad, shift_two_grad, down_bias_grad = (
        lax.psum(
            (
                gain_one_grad,
                shift_one_grad,
                out_bias_grad,
                gain_two_grad,
                shift_two_grad,
                down_bias_grad,
            ),
            ("dp", "mp"),
        )
    )
    return (
        layer_out,
        input_grad,
        gain_one_grad,
        shift_one_grad,
        query_weight_grad,
        query_bias_grad,
        key_weight_grad,
        value_weight_grad,
        value_bias_grad,
        out_weight_grad,
        out_bias_grad,
        gain_two_grad,
        shift_two_grad,
        up_weight_grad,
        up_bias_grad,
        down_weight_grad,
        down_bias_grad,
    )


def solution(mesh):
    in_specs = (
        P(("dp", "mp"), None),
        P("dp"),
        P("dp", None),
        P(),
        P(),
        P(None, "mp"),
        P("mp"),
        P(None, "mp"),
        P(None, "mp"),
        P("mp"),
        P("mp", None),
        P(),
        P(),
        P(),
        P(None, "mp"),
        P("mp"),
        P("mp", None),
        P(),
        P(("dp", "mp"), None),
    )
    out_specs = (
        P(("dp", "mp"), None),
        P(("dp", "mp"), None),
        P(),
        P(),
        P(None, "mp"),
        P("mp"),
        P(None, "mp"),
        P(None, "mp"),
        P("mp"),
        P("mp", None),
        P(),
        P(),
        P(),
        P(None, "mp"),
        P("mp"),
        P("mp", None),
        P(),
    )
    return jax.shard_map(
        per_device, mesh=mesh, in_specs=in_specs, out_specs=out_specs, check_vma=False
    )
```

profile of v0, /device:TPU:0, one launch (start us, length us, event | category | flops | bytes accessed | tf_op | source)
XLA Modules:
  0.0 535.1 jit_solution(10001136210454369403)
XLA Ops:
  11.7 2.0 fusion.43
  15.1 1.4 broadcast_compare_fusion
  17.6 18.7 %all-gather.5.cloned.1.call-done = bf16[1024,768]{1,0:T(8,128)(2,1)} async-done(((bf16[256,768]{1,0:T(8,128)(2,1)}), bf16[1024,768]{1,0:T(8,128)(2,1)}) %all-gather.5.cloned.1.call-update) | async-done | bytes 1572880 | tf_op jit(solution)/shard_map/all_gather | solution.py:64
  36.2 2.3 fusion.27
  39.3 1.4 fusion.65
  40.7 1.5 fusion
  43.3 1.6 fusion.35
  45.0 1.4 fusion.64
  46.5 1.5 fusion.1
  49.7 1.7 fusion.34
  52.0 1.8 convolution_convert_fusion.2
  58.1 23.9 %reduce-scatter.5.cloned.1.call-done = bf16[256,768]{1,0:T(8,128)(2,1)} async-done(((bf16[1024,768]{1,0:T(8,128)(2,1)}), bf16[256,768]{1,0:T(8,128)(2,1)}) %reduce-scatter.5.cloned.1.call-update) | async-done | bytes 393232 | tf_op jit(solution)/shard_map/reduce_scatter | solution.py:94
  83.3 1.3 multiply_reduce_fusion.2
  85.9 2.0 add_convert_fusion.3
  88.0 1.6 fusion.37
  90.8 16.9 %all-gather.7.cloned.1.call-done = bf16[1024,768]{1,0:T(8,128)(2,1)} async-done(((bf16[256,768]{1,0:T(8,128)(2,1)}), bf16[1024,768]{1,0:T(8,128)(2,1)}) %all-gather.7.cloned.1.call-update) | async-done | bytes 1572880 | tf_op jit(solution)/shard_map/all_gather | solution.py:102
  107.7 4.8 fusion.66
  112.5 16.9 %all-gather.9.cloned.1.call-done = bf16[1024,768]{1,0:T(8,128)(2,1)} async-done(((bf16[256,768]{1,0:T(8,128)(2,1)}), bf16[1024,768]{1,0:T(8,128)(2,1)}) %all-gather.9.cloned.1.call-update) | async-done | bytes 1572880 | tf_op jit(solution)/shard_map/all_gather | solution.py:115
  129.4 11.8 %convert_reduce_fusion = (f32[768]{0:T(1024)}, bf16[1024,768]{1,0:T(8,128)(2,1)S(1)}, f32[1024,768]{1,0:T(8,128)}) fusion(f32[1024,768]{1,0:T(8,128)} %fusion.66, f32[768]{0:T(1024)S(1)} %convert_element_type.170, bf16[1024,768]{1,0:T(8,128)(2,1)} %all-gather.9.cloned.1.call-done, bf16[768,768]{1,0:T(8,128)(2,1)S(1)} %copy-done), kind=kOutput, calls=%fused_computation.20 | convolution fusion | flops 1266941184 | bytes 10622976 | tf_op jit(solution)/shard_map/rd,fd->rf/dot_general | solution.py:117
  142.4 2.6 convolution_convert_fusion
  145.0 3.3 multiply_convert_fusion.2
  149.5 2.5 convolution_convert_fusion.1
  152.1 1.4 convert_element_type.174
  153.5 19.7 %reduce-scatter.9.cloned.1.call-done = bf16[256,768]{1,0:T(8,128)(2,1)} async-done(((bf16[1024,768]{1,0:T(8,128)(2,1)}), bf16[256,768]{1,0:T(8,128)(2,1)}) %reduce-scatter.9.cloned.1.call-update) | async-done | bytes 393232 | tf_op jit(solution)/shard_map/reduce_scatter | solution.py:124
  173.1 2.1 fusion.47
  176.5 27.7 %reduce-scatter.7.cloned.1.call-done = bf16[256,768]{1,0:T(8,128)(2,1)} async-done(((bf16[1024,768]{1,0:T(8,128)(2,1)}), bf16[256,768]{1,0:T(8,128)(2,1)}) %reduce-scatter.7.cloned.1.call-update) | async-done | bytes 393232 | tf_op jit(solution)/shard_map/reduce_scatter | solution.py:105
  204.2 2.6 fusion.59
  206.8 2.4 fusion.36
  210.8 18.1 %all-gather.11.cloned.1.call-done = bf16[1024,768]{1,0:T(8,128)(2,1)} async-done(((bf16[256,768]{1,0:T(8,128)(2,1)}), bf16[1024,768]{1,0:T(8,128)(2,1)}) %all-gather.11.cloned.1.call-update) | async-done | bytes 1572880 | tf_op jit(solution)/shard_map/all_gather | solution.py:137
  229.0 2.1 convolution_convert_fusion.3
  231.1 3.9 multiply_reduce_fusion.1
  235.8 1.4 multiply_convert_fusion.1
  240.2 1.9 multiply_reduce_fusion
  242.1 1.8 convert_reduce_fusion.4
  244.0 1.4 multiply_convert_fusion
  249.6 1.8 add_convert_fusion
  251.7 4.9 fusion.71
  256.6 2.8 fusion.70
  265.5 22.2 %all-reduce.1 = (f32[192]{0:T(256)}, f32[192]{0:T(256)}, f32[768]{0:T(1024)}) all-reduce(f32[192]{0:T(256)S(1)} %reduce_sum.217, f32[192]{0:T(256)S(1)} %reduce_sum.219, f32[768]{0:T(1024)S(1)} %copy-done.58), channel_id=1, replica_groups=mesh['dp'=8,'mp'=4] {'dp'}, use_global_device_ids=true, to_apply=%region_24.25 | all-reduce | flops 1152 | bytes 9216 | tf_op jit(solution)/shard_map/psum | solution.py:211
  289.0 1.5 fusion.48
  290.6 41.8 %all-reduce = (f32[768]{0:T(1024)}, f32[768]{0:T(1024)}, f32[768]{0:T(1024)}, f32[768]{0:T(1024)}, f32[768]{0:T(1024)}, /*index=5*/f32[768]{0:T(1024)}) all-reduce(f32[768]{0:T(1024)S(1)} %get-tuple-element.19, f32[768]{0:T(1024)S(1)} %get-tuple-element.24, f32[768]{0:T(1024)S(1)} %copy-done.50, ...), channel_id=1, replica_groups=mesh['dp'=8,'mp'=4] {'dp','mp'}, use_global_device_ids=true, to_apply=%region_19.20 | all-reduce | flops 4608 | bytes 36864 | tf_op jit(solution)/shard_map/psum | solution.py:226
  332.3 2.3 add_add_fusion.2
  334.6 184.2 %all-reduce.5.cloned.1.call-done = (f32[768,192]{0,1:T(8,128)}, f32[768,192]{0,1:T(8,128)}, f32[768,192]{0,1:T(8,128)}, f32[192,768]{1,0:T(8,128)}, f32[768,768]{1,0:T(8,128)}, /*index=5*/f32[768,768]{1,0:T(8,128)}) async-done(((f32[768,192]{0,1:T(8,128)}, f32[768,192]{0,1:T(8,128)}, f32[768,192]{0,1:T(8,128)}, f32[192,768]{1,0:T(8,128)}, f32[768,768]{1,0:T(8,128)}, /*index=5*/f32[768,768]{1,0:T(8,128)}), ...) | async-done | bytes 7077904 | tf_op jit(solution)/shard_map/psum | solution.py:211
  518.8 2.1 copy.42
  520.9 1.9 copy.43
  522.8 1.9 copy.44
  525.6 1.4 copy.46
  527.0 1.4 copy.47
  (202 shorter events, 40.8 us)
Async XLA Ops:
  7.2 122.2 %copy-start = (bf16[768,768]{1,0:T(8,128)(2,1)S(1)}, bf16[768,768]{1,0:T(8,128)(2,1)}, u32[]{:S(2)}) copy-start(bf16[768,768]{1,0:T(8,128)(2,1)} %param.35) | copy-start | bytes 3538948
  7.2 29.0 %all-gather.5.cloned.1.call-start = ((), (), s32[]{:S(2)}) async-start(), calls=%async_computation.4 | async-start | bytes 1966080 | tf_op jit(solution)/shard_map/all_gather | solution.py:64
  8.5 6.0 %copy-start.40 = (f32[256]{0:T(256)}, f32[256]{0:T(256)S(1)}, u32[]{:S(2)}) copy-start(f32[256]{0:T(256)S(1)} %broadcast_multiply_fusion.1) | copy-start | bytes 3076
  10.3 4.1 copy-start.45
  11.0 3.4 copy-start.37
  13.7 68.3 %reduce-scatter.5.cloned.1.call-start = ((), (), s32[]{:S(2)}) async-start(), calls=%async_computation.5 | async-start | bytes 1966080 | tf_op jit(solution)/shard_map/reduce_scatter | solution.py:94
  15.1 23.4 %copy-start.34 = (bf16[768,192]{0,1:T(8,128)(2,1)S(1)}, bf16[768,192]{0,1:T(8,128)(2,1)}, u32[]{:S(2)}) copy-start(bf16[768,192]{0,1:T(8,128)(2,1)} %param.26) | copy-start | bytes 884740
  36.2 3.0 copy-start.19
  38.6 6.5 %copy-start.16 = (bf16[512,192]{0,1:T(8,128)(2,1)}, bf16[512,192]{0,1:T(8,128)(2,1)S(1)}, u32[]{:S(2)}) copy-start(bf16[512,192]{0,1:T(8,128)(2,1)S(1)} %get-tuple-element.55) | copy-start | bytes 589828
  39.2 5.8 %copy-start.7 = (bf16[1024,192]{0,1:T(8,128)(2,1)}, bf16[1024,192]{0,1:T(8,128)(2,1)S(1)}, u32[]{:S(2)}) copy-start(bf16[1024,192]{0,1:T(8,128)(2,1)S(1)} %convolution_convert_fusion.4) | copy-start | bytes 1179652
  42.9 5.1 copy-start.22
  45.0 6.4 %copy-start.26 = (bf16[3,64,512]{2,1,0:T(8,128)(2,1)}, bf16[3,64,512]{2,1,0:T(8,128)(2,1)S(1)}, u32[]{:S(2)}) copy-start(bf16[3,64,512]{2,1,0:T(8,128)(2,1)S(1)} %fusion.35) | copy-start | bytes 589828
  51.4 3.3 copy-start.59
  51.4 30.7 %copy-start.4 = (bf16[256,768]{1,0:T(8,128)(2,1)S(1)}, bf16[256,768]{1,0:T(8,128)(2,1)}, u32[]{:S(2)}) copy-start(bf16[256,768]{1,0:T(8,128)(2,1)} %param.19) | copy-start | bytes 1179652
  52.0 35.9 %copy-start.11 = (bf16[256,768]{1,0:T(8,128)(2,1)S(1)}, bf16[256,768]{1,0:T(8,128)(2,1)}, u32[]{:S(2)}) copy-start(bf16[256,768]{1,0:T(8,128)(2,1)} %param.37) | copy-start | bytes 1179652
  53.8 53.9 %all-gather.7.cloned.1.call-start = ((), (), s32[]{:S(2)}) async-start(), calls=%async_computation.6 | async-start | bytes 1966080 | tf_op jit(solution)/shard_map/all_gather | solution.py:102
  87.9 41.4 %all-gather.9.cloned.1.call-start = ((), (), s32[]{:S(2)}) async-start(), calls=%async_computation.8 | async-start | bytes 1966080 | tf_op jit(solution)/shard_map/all_gather | solution.py:115
  89.6 83.6 %reduce-scatter.9.cloned.1.call-start = ((), (), s32[]{:S(2)}) async-start(), calls=%async_computation.9 | async-start | bytes 1966080 | tf_op jit(solution)/shard_map/reduce_scatter | solution.py:124
  129.4 13.0 %copy-start.61 = (bf16[768,768]{1,0:T(8,128)(2,1)S(1)}, bf16[768,768]{1,0:T(8,128)(2,1)}, u32[]{:S(2)}) copy-start(bf16[768,768]{1,0:T(8,128)(2,1)} %param.33) | copy-start | bytes 3538948
  145.0 59.2 %reduce-scatter.7.cloned.1.call-start = ((), (), s32[]{:S(2)}) async-start(), calls=%async_computation.7 | async-start | bytes 1966080 | tf_op jit(solution)/shard_map/reduce_scatter | solution.py:105
  149.5 23.7 %copy-start.6 = (bf16[256,768]{1,0:T(8,128)(2,1)S(1)}, bf16[256,768]{1,0:T(8,128)(2,1)}, u32[]{:S(2)}) copy-start(bf16[256,768]{1,0:T(8,128)(2,1)} %reduce-scatter.5.cloned.1.call-done) | copy-start | bytes 1179652
  152.0 54.8 %copy-start.12 = (bf16[256,768]{1,0:T(8,128)(2,1)S(1)}, bf16[256,768]{1,0:T(8,128)(2,1)}, u32[]{:S(2)}) copy-start(bf16[256,768]{1,0:T(8,128)(2,1)} %param.37) | copy-start | bytes 1179652
  152.0 76.9 %all-gather.11.cloned.1.call-start = ((), (), s32[]{:S(2)}) async-start(), calls=%async_computation.10 | async-start | bytes 1966080 | tf_op jit(solution)/shard_map/all_gather | solution.py:137
  206.8 24.3 %copy-start.23 = (bf16[1024,192]{0,1:T(8,128)(2,1)S(1)}, bf16[1024,192]{0,1:T(8,128)(2,1)}, u32[]{:S(2)}) copy-start(bf16[1024,192]{0,1:T(8,128)(2,1)} %copy-done.22) | copy-start | bytes 1179652
  209.2 78.5 %reduce-scatter.11.cloned.1.call-start = ((), (), s32[]{:S(2)}) async-start(), calls=%async_computation.11 | async-start | bytes 1966080 | tf_op jit(solution)/shard_map/reduce_scatter | solution.py:189
  231.1 4.0 slice-start
  231.1 4.7 slice-start.1
  235.1 3.9 slice-start.2
  235.8 3.2 slice-start.3
  251.4 267.4 %all-reduce.5.cloned.1.call-start = ((), (), s32[]{:S(2)}) async-start(), calls=%async_computation.12 | async-start | bytes 14155776 | tf_op jit(solution)/shard_map/psum | solution.py:211
  251.7 4.9 copy-start.60
  251.7 4.9 copy-start.63
  256.6 2.9 copy-start.25
  256.6 2.9 copy-start.27
  256.6 2.9 copy-start.29
  264.7 23.0 %copy-start.38 = (f32[768]{0:T(1024)S(1)}, f32[768]{0:T(1024)}, u32[]{:S(2)}) copy-start(f32[768]{0:T(1024)} %copy-done.37) | copy-start | bytes 9220
  264.7 23.0 %copy-start.41 = (f32[256]{0:T(256)S(1)}, f32[256]{0:T(256)}, u32[]{:S(2)}) copy-start(f32[256]{0:T(256)} %copy-done.40) | copy-start | bytes 3076
  264.7 24.3 %copy-start.55 = (f32[256]{0:T(256)S(1)}, f32[256]{0:T(256)}, u32[]{:S(2)}) copy-start(f32[256]{0:T(256)} %copy-done.54) | copy-start | bytes 3076
  264.7 24.3 %copy-start.46 = (f32[256]{0:T(256)S(1)}, f32[256]{0:T(256)}, u32[]{:S(2)}) copy-start(f32[256]{0:T(256)} %copy-done.45) | copy-start | bytes 3076
  264.7 25.8 %copy-start.47 = (f32[768]{0:T(1024)S(1)}, f32[768]{0:T(1024)}, u32[]{:S(2)}) copy-start(f32[768]{0:T(1024)} %get-tuple-element.17) | copy-start | bytes 9220
  264.7 25.8 %copy-start.48 = (f32[768]{0:T(1024)S(1)}, f32[768]{0:T(1024)}, u32[]{:S(2)}) copy-start(f32[768]{0:T(1024)} %get-tuple-element.23) | copy-start | bytes 9220
  264.7 25.8 %copy-start.49 = (f32[768]{0:T(1024)S(1)}, f32[768]{0:T(1024)}, u32[]{:S(2)}) copy-start(f32[768]{0:T(1024)} %get-tuple-element.21) | copy-start | bytes 9220
  264.7 25.8 %copy-start.50 = (f32[768]{0:T(1024)S(1)}, f32[768]{0:T(1024)}, u32[]{:S(2)}) copy-start(f32[768]{0:T(1024)} %get-tuple-element.22) | copy-start | bytes 9220
  264.7 67.6 %copy-start.13 = (bf16[256,768]{1,0:T(8,128)(2,1)S(1)}, bf16[256,768]{1,0:T(8,128)(2,1)}, u32[]{:S(2)}) copy-start(bf16[256,768]{1,0:T(8,128)(2,1)} %param.37) | copy-start | bytes 1179652
  264.8 67.6 %copy-start.53 = (f32[256]{0:T(256)S(1)}, f32[256]{0:T(256)}, u32[]{:S(2)}) copy-start(f32[256]{0:T(256)} %copy-done.52) | copy-start | bytes 3076
  518.8 5.9 %copy-start.30 = (f32[192,768]{1,0:T(8,128)S(1)}, f32[192,768]{1,0:T(8,128)}, u32[]{:S(2)}) copy-start(f32[192,768]{1,0:T(8,128)} %get-tuple-element.77) | copy-start | bytes 1769476
  518.8 6.7 %copy-start.15 = (f32[768,768]{1,0:T(8,128)S(1)}, f32[768,768]{1,0:T(8,128)}, u32[]{:S(2)}) copy-start(f32[768,768]{1,0:T(8,128)} %get-tuple-element.81) | copy-start | bytes 7077892
  525.6 2.8 copy-start.1
  (29 other events, 45.4 us)
Sparse Core Ops, SparseCore 0:
  13.8 22.3 all-gather.4
  54.0 28.0 reduce-scatter.4
  88.0 19.6 all-gather.6
  109.7 19.6 all-gather.8
  145.1 27.9 reduce-scatter.8
  176.1 28.0 reduce-scatter.6
  209.3 19.6 all-gather.10
  251.6 27.9 reduce-scatter.10
  285.8 232.9 all-reduce.4
where the time goes:
time: 544 us; the launch traced here: 535 us
  waiting for transfers between devices  326 us (60%)
  matrix products  64.6 us (12%)
  blocking collectives  63.9 us (12%)
  other arithmetic  42.8 us (8%)
  local copies, waits for them, and re-layouts  21.6 us (4%)
  between operations  14.8 us (3%)
    psum x1, waiting for transfers between devices, per_device(): lax.psum((query_weight_grad, query_bias_grad, key_weight_grad, value_weig...  184 us
    psum x1, blocking collectives, per_device(): lax.psum((gain_one_grad, shift_one_grad, out_bias_grad, gain_two_grad, sh...  41.8 us
    reduce_scatter x1, waiting for transfers between devices, per_device(): lax.psum_scatter(jnp.dot(activated, down_weight, preferred_element_type=f...  27.7 us
    reduce_scatter x1, waiting for transfers between devices, per_device(): lax.psum_scatter(jnp.dot(context, out_weight, preferred_element_type=f32)...  23.9 us
    psum x1, blocking collectives, per_device(): lax.psum((query_weight_grad, query_bias_grad, key_weight_grad, value_weig...  22.2 us
    reduce_scatter x1, waiting for transfers between devices, per_device(): lax.psum_scatter(jnp.einsum('rf,df->rd', hidden_grad, up_weight, preferre...  19.7 us
    unnamed x142, local copies, waits for them, and re-layouts  18.9 us
    all_gather x1, waiting for transfers between devices, per_device(): normed_all = lax.all_gather(normed, 'mp', axis=0, tiled=True)  18.7 us
  transfers between devices with their start and end apart: 9, of which 8 were waited for; matrix products, arithmetic and copies ran while one was open for 8% of the time, Pallas kernels for 0%

commit v1 on v0

--- a/solution.py
+++ b/solution.py
@@ -112,7 +112,25 @@
     out_grad = cotangent.astype(f32)
     mlp_grad = out_grad * keep_rows[:, 1:2]
     down_bias_grad = jnp.sum(mlp_grad, axis=0)
-    mlp_grad_all = lax.all_gather(mlp_grad.astype(bf16), "mp", axis=0, tiled=True)
+    array = mlp_grad.astype(bf16)
+    size, position, span = (lax.axis_size("mp"), lax.axis_index("mp"), array.shape[0])
+    right = [(i, (i + 1) % size) for i in range(size)]
+    downward = [(i, (i - 1) % size) for i in range(size)]
+    filled = jnp.zeros((*array.shape[:0], size * span, *array.shape[0 + 1 :]), array.dtype)
+    filled = lax.dynamic_update_slice_in_dim(filled, array, position * span, axis=0)
+    from_left = from_right = array
+    half = size // 2
+    for turn in range(1, half + 1):
+        from_left = lax.ppermute(from_left, "mp", right)
+        filled = lax.dynamic_update_slice_in_dim(
+            filled, from_left, (position - turn) % size * span, axis=0
+        )
+        if turn < size - half:
+            from_right = lax.ppermute(from_right, "mp", downward)
+            filled = lax.dynamic_update_slice_in_dim(
+                filled, from_right, (position + turn) % size * span, axis=0
+            )
+    mlp_grad_all = filled
     down_weight_grad = jnp.einsum("rf,rd->fd", activated, mlp_grad_all, preferred_element_type=f32)
     act_grad = jnp.einsum("rd,fd->rf", mlp_grad_all, down_weight, preferred_element_type=f32)
     unused_value, gelu_pull = jax.vjp(gelu_exact, hidden)

time: 544 us -> 525 us (0.965); the launches traced: 535 us -> 524 us
  waiting for transfers between devices: 326 us -> 311 us
  local copies, waits for them, and re-layouts: 21.6 us -> 27.1 us
    ppermute x0 -> x3, waiting for transfers between devices: none -> 18.8 us  [the longest x2 18.6 us: per_device(): from_left = lax.ppermute(from_left, 'mp', right)]
    all_gather x1, waiting for transfers between devices: 16.9 us -> 0.01 us  [per_device(): normed_two_all = lax.all_gather(normed_two, 'mp', axis=0, tiled=True)]
    all_gather x1 -> x0, waiting for transfers between devices: 16.9 us -> none  [per_device(): lax.all_gather(mlp_grad.astype(bf16), 'mp', axis=0, tiled=True)]
    unnamed x142 -> x150, local copies, waits for them, and re-layouts: 18.9 us -> 20 us
  transfers between devices with their start and end apart: 9 -> 11, of which waited for: 8 -> 9; matrix products, arithmetic and copies ran while one was open for 8% -> 9% of each run, Pallas kernels for 0% -> 0%
where the time goes in v1:
time: 525 us; the launch traced here: 524 us
  waiting for transfers between devices  311 us (59%)
  blocking collectives  63.9 us (12%)
  matrix products  61.5 us (12%)
  other arithmetic  43.4 us (8%)
  local copies, waits for them, and re-layouts  27.1 us (5%)
  between operations  15 us (3%)
    psum x1, waiting for transfers between devices, per_device(): lax.psum((query_weight_grad, query_bias_grad, key_weight_grad, value_weig...  184 us
    psum x1, blocking collectives, per_device(): lax.psum((gain_one_grad, shift_one_grad, out_bias_grad, gain_two_grad, sh...  41.7 us
    reduce_scatter x1, waiting for transfers between devices, per_device(): lax.psum_scatter(jnp.dot(activated, down_weight, preferred_element_type=f...  27.1 us
    reduce_scatter x1, waiting for transfers between devices, per_device(): lax.psum_scatter(jnp.dot(context, out_weight, preferred_element_type=f32)...  23.8 us
    psum x1, blocking collectives, per_device(): lax.psum((query_weight_grad, query_bias_grad, key_weight_grad, value_weig...  22.2 us
    unnamed x150, local copies, waits for them, and re-layouts  20 us
    reduce_scatter x1, waiting for transfers between devices, per_device(): lax.psum_scatter(jnp.einsum('rf,df->rd', hidden_grad, up_weight, preferre...  19.7 us
    all_gather x1, waiting for transfers between devices, per_device(): normed_all = lax.all_gather(normed, 'mp', axis=0, tiled=True)  18.7 us
  transfers between devices with their start and end apart: 11, of which 9 were waited for; matrix products, arithmetic and copies ran while one was open for 9% of the time, Pallas kernels for 0%

profile of v1, /device:TPU:0, one launch (start us, length us, event | category | flops | bytes accessed | tf_op | source)
XLA Modules:
  0.0 523.9 jit_solution(11726729894433210002)
XLA Ops:
  11.7 2.0 fusion.43
  15.1 1.4 broadcast_compare_fusion
  17.5 18.7 %all-gather.4.cloned.1.call-done = bf16[1024,768]{1,0:T(8,128)(2,1)} async-done(((bf16[256,768]{1,0:T(8,128)(2,1)}), bf16[1024,768]{1,0:T(8,128)(2,1)}) %all-gather.4.cloned.1.call-update) | async-done | bytes 1572880 | tf_op jit(solution)/shard_map/all_gather | solution.py:64
  36.2 2.3 fusion.27
  39.2 1.4 fusion.66
  40.7 1.5 fusion
  43.3 1.6 fusion.35
  45.0 1.4 fusion.65
  46.5 1.5 fusion.1
  49.7 1.6 fusion.34
  52.0 1.8 convolution_convert_fusion.2
  58.1 23.8 %reduce-scatter.5.cloned.1.call-done = bf16[256,768]{1,0:T(8,128)(2,1)} async-done(((bf16[1024,768]{1,0:T(8,128)(2,1)}), bf16[256,768]{1,0:T(8,128)(2,1)}) %reduce-scatter.5.cloned.1.call-update) | async-done | bytes 393232 | tf_op jit(solution)/shard_map/reduce_scatter | solution.py:94
  85.7 2.0 add_convert_fusion.3
  88.0 1.6 constant_dynamic-update-slice_fusion.3
  90.7 1.7 collective-permute-start.1
  92.4 13.2 %collective-permute-done = bf16[256,768]{1,0:T(8,128)(2,1)S(1)} collective-permute-done((bf16[256,768]{1,0:T(8,128)(2,1)}, bf16[256,768]{1,0:T(8,128)(2,1)S(1)}, u32[]{:S(2)}, u32[]{:S(2)}) %collective-permute-start) | collective-permute-done | bytes 393248 | tf_op jit(solution)/shard_map/ppermute | solution.py:124
  107.9 1.8 constant_dynamic-update-slice_fusion.1
  109.6 5.4 %collective-permute-done.2 = bf16[256,768]{1,0:T(8,128)(2,1)} collective-permute-done((bf16[256,768]{1,0:T(8,128)(2,1)S(1)}, bf16[256,768]{1,0:T(8,128)(2,1)}, u32[]{:S(2)}, u32[]{:S(2)}) %collective-permute-start.2) | collective-permute-done | bytes 393248 | tf_op jit(solution)/shard_map/ppermute | solution.py:124
  115.0 1.8 constant_dynamic-update-slice_fusion
  116.8 3.3 fusion.67
  120.1 10.3 %convert_reduce_fusion = (f32[768]{0:T(1024)}, bf16[1024,768]{1,0:T(8,128)(2,1)S(1)}, f32[1024,768]{1,0:T(8,128)}) fusion(f32[1024,768]{1,0:T(8,128)S(1)} %fusion.67, f32[768]{0:T(1024)S(1)} %copy-done.48, bf16[1024,768]{1,0:T(8,128)(2,1)S(1)} %copy-done.28, bf16[768,768]{1,0:T(8,128)(2,1)S(1)} %copy-done), kind=kOutput, calls=%fused_computation.20 | convolution fusion | flops 1266941184 | bytes 10622976 | tf_op jit(solution)/shard_map/rd,fd->rf/dot_general | solution.py:135
  131.6 2.6 convolution_convert_fusion
  134.3 3.3 multiply_convert_fusion.2
  138.7 2.6 convolution_convert_fusion.1
  141.3 1.4 convert_element_type.174
  142.7 19.7 %reduce-scatter.9.cloned.1.call-done = bf16[256,768]{1,0:T(8,128)(2,1)} async-done(((bf16[1024,768]{1,0:T(8,128)(2,1)}), bf16[256,768]{1,0:T(8,128)(2,1)}) %reduce-scatter.9.cloned.1.call-update) | async-done | bytes 393232 | tf_op jit(solution)/shard_map/reduce_scatter | solution.py:142
  162.4 2.1 fusion.47
  165.7 27.1 %reduce-scatter.7.cloned.1.call-done = bf16[256,768]{1,0:T(8,128)(2,1)} async-done(((bf16[1024,768]{1,0:T(8,128)(2,1)}), bf16[256,768]{1,0:T(8,128)(2,1)}) %reduce-scatter.7.cloned.1.call-update) | async-done | bytes 393232 | tf_op jit(solution)/shard_map/reduce_scatter | solution.py:105
  192.8 2.6 fusion.59
  195.4 2.4 fusion.36
  199.5 18.1 %all-gather.8.cloned.1.call-done = bf16[1024,768]{1,0:T(8,128)(2,1)} async-done(((bf16[256,768]{1,0:T(8,128)(2,1)}), bf16[1024,768]{1,0:T(8,128)(2,1)}) %all-gather.8.cloned.1.call-update) | async-done | bytes 1572880 | tf_op jit(solution)/shard_map/all_gather | solution.py:155
  217.6 2.1 convolution_convert_fusion.3
  219.8 3.9 multiply_reduce_fusion.1
  228.8 1.9 multiply_reduce_fusion
  230.8 1.8 convert_reduce_fusion.4
  238.2 1.8 add_convert_fusion
  240.4 4.9 fusion.72
  245.3 2.8 fusion.71
  254.2 22.2 %all-reduce.1 = (f32[192]{0:T(256)}, f32[192]{0:T(256)}, f32[768]{0:T(1024)}) all-reduce(f32[192]{0:T(256)S(1)} %reduce_sum.217, f32[192]{0:T(256)S(1)} %reduce_sum.219, f32[768]{0:T(1024)S(1)} %copy-done.62), channel_id=1, replica_groups=mesh['dp'=8,'mp'=4] {'dp'}, use_global_device_ids=true, to_apply=%region_24.25 | all-reduce | flops 1152 | bytes 9216 | tf_op jit(solution)/shard_map/psum | solution.py:229
  277.7 1.5 fusion.48
  279.2 41.7 %all-reduce = (f32[768]{0:T(1024)}, f32[768]{0:T(1024)}, f32[768]{0:T(1024)}, f32[768]{0:T(1024)}, f32[768]{0:T(1024)}, /*index=5*/f32[768]{0:T(1024)}) all-reduce(f32[768]{0:T(1024)S(1)} %get-tuple-element.19, f32[768]{0:T(1024)S(1)} %get-tuple-element.24, f32[768]{0:T(1024)S(1)} %copy-done.54, ...), channel_id=1, replica_groups=mesh['dp'=8,'mp'=4] {'dp','mp'}, use_global_device_ids=true, to_apply=%region_19.20 | all-reduce | flops 4608 | bytes 36864 | tf_op jit(solution)/shard_map/psum | solution.py:244
  321.0 2.3 add_add_fusion.2
  323.2 184.2 %all-reduce.5.cloned.1.call-done = (f32[768,192]{0,1:T(8,128)}, f32[768,192]{0,1:T(8,128)}, f32[768,192]{0,1:T(8,128)}, f32[192,768]{1,0:T(8,128)}, f32[768,768]{1,0:T(8,128)}, /*index=5*/f32[768,768]{1,0:T(8,128)}) async-done(((f32[768,192]{0,1:T(8,128)}, f32[768,192]{0,1:T(8,128)}, f32[768,192]{0,1:T(8,128)}, f32[192,768]{1,0:T(8,128)}, f32[768,768]{1,0:T(8,128)}, /*index=5*/f32[768,768]{1,0:T(8,128)}), ...) | async-done | bytes 7077904 | tf_op jit(solution)/shard_map/psum | solution.py:229
  507.5 2.1 copy.46
  509.5 1.9 copy.47
  511.5 1.9 copy.48
  514.2 1.4 copy.50
  515.6 1.4 copy.51
  (217 shorter events, 47.2 us)
Async XLA Ops:
  7.2 112.9 %copy-start = (bf16[768,768]{1,0:T(8,128)(2,1)S(1)}, bf16[768,768]{1,0:T(8,128)(2,1)}, u32[]{:S(2)}) copy-start(bf16[768,768]{1,0:T(8,128)(2,1)} %param.35) | copy-start | bytes 3538948
  7.2 29.0 %all-gather.4.cloned.1.call-start = ((), (), s32[]{:S(2)}) async-start(), calls=%async_computation.4 | async-start | bytes 1966080 | tf_op jit(solution)/shard_map/all_gather | solution.py:64
  8.5 5.9 %copy-start.43 = (f32[256]{0:T(256)}, f32[256]{0:T(256)S(1)}, u32[]{:S(2)}) copy-start(f32[256]{0:T(256)S(1)} %broadcast_multiply_fusion.1) | copy-start | bytes 3076
  10.3 4.1 copy-start.49
  11.0 3.4 copy-start.40
  13.7 68.3 %reduce-scatter.5.cloned.1.call-start = ((), (), s32[]{:S(2)}) async-start(), calls=%async_computation.5 | async-start | bytes 1966080 | tf_op jit(solution)/shard_map/reduce_scatter | solution.py:94
  15.1 23.4 %copy-start.37 = (bf16[768,192]{0,1:T(8,128)(2,1)S(1)}, bf16[768,192]{0,1:T(8,128)(2,1)}, u32[]{:S(2)}) copy-start(bf16[768,192]{0,1:T(8,128)(2,1)} %param.26) | copy-start | bytes 884740
  38.5 6.5 %copy-start.17 = (bf16[512,192]{0,1:T(8,128)(2,1)}, bf16[512,192]{0,1:T(8,128)(2,1)S(1)}, u32[]{:S(2)}) copy-start(bf16[512,192]{0,1:T(8,128)(2,1)S(1)} %get-tuple-element.57) | copy-start | bytes 589828
  39.2 5.8 %copy-start.7 = (bf16[1024,192]{0,1:T(8,128)(2,1)}, bf16[1024,192]{0,1:T(8,128)(2,1)S(1)}, u32[]{:S(2)}) copy-start(bf16[1024,192]{0,1:T(8,128)(2,1)S(1)} %convolution_convert_fusion.4) | copy-start | bytes 1179652
  42.9 5.1 copy-start.23
  45.0 6.4 %copy-start.29 = (bf16[3,64,512]{2,1,0:T(8,128)(2,1)}, bf16[3,64,512]{2,1,0:T(8,128)(2,1)S(1)}, u32[]{:S(2)}) copy-start(bf16[3,64,512]{2,1,0:T(8,128)(2,1)S(1)} %fusion.35) | copy-start | bytes 589828
  51.3 3.3 copy-start.63
  51.3 30.6 %copy-start.4 = (bf16[256,768]{1,0:T(8,128)(2,1)S(1)}, bf16[256,768]{1,0:T(8,128)(2,1)}, u32[]{:S(2)}) copy-start(bf16[256,768]{1,0:T(8,128)(2,1)} %param.19) | copy-start | bytes 1179652
  53.8 34.2 %copy-start.11 = (bf16[256,768]{1,0:T(8,128)(2,1)S(1)}, bf16[256,768]{1,0:T(8,128)(2,1)}, u32[]{:S(2)}) copy-start(bf16[256,768]{1,0:T(8,128)(2,1)} %param.37) | copy-start | bytes 1179652
  53.8 63.0 %all-gather.6.cloned.1.call-start = ((), (), s32[]{:S(2)}) async-start(), calls=%async_computation.6 | async-start | bytes 1966080 | tf_op jit(solution)/shard_map/all_gather | solution.py:102
  87.8 74.6 %reduce-scatter.9.cloned.1.call-start = ((), (), s32[]{:S(2)}) async-start(), calls=%async_computation.8 | async-start | bytes 1966080 | tf_op jit(solution)/shard_map/reduce_scatter | solution.py:142
  90.7 14.9 %collective-permute-start = (bf16[256,768]{1,0:T(8,128)(2,1)}, bf16[256,768]{1,0:T(8,128)(2,1)S(1)}, u32[]{:S(2)}, u32[]{:S(2)}) collective-permute-start(bf16[256,768]{1,0:T(8,128)(2,1)} %get-tuple-element.49), channel_id=1, source_target_pairs={{0,1},{1,2},{2,3},{3,0},{4,5},{5,6},{6,7},{7,4},{8,9},{9,10},{10,1... | collective-permute-start | bytes 1179656 | tf_op jit(solution)/shard_map/ppermute | solution.py:124
  90.7 17.2 %collective-permute-start.1 = (bf16[256,768]{1,0:T(8,128)(2,1)}, bf16[256,768]{1,0:T(8,128)(2,1)}, u32[]{:S(2)}, u32[]{:S(2)}) collective-permute-start(bf16[256,768]{1,0:T(8,128)(2,1)} %get-tuple-element.49), channel_id=1, source_target_pairs={{0,3},{1,0},{2,1},{3,2},{4,7},{5,4},{6,5},{7,6},{8,11},{9,8},{10,9... | collective-permute-start | bytes 1179656 | tf_op jit(solution)/shard_map/ppermute | solution.py:129
  105.6 9.4 %collective-permute-start.2 = (bf16[256,768]{1,0:T(8,128)(2,1)S(1)}, bf16[256,768]{1,0:T(8,128)(2,1)}, u32[]{:S(2)}, u32[]{:S(2)}) collective-permute-start(bf16[256,768]{1,0:T(8,128)(2,1)S(1)} %collective-permute-done), channel_id=1, source_target_pairs={{0,1},{1,2},{2,3},{3,0},{4,5},{5,6},{6,7},{7,4},{8,9},{9,10},{10,1... | collective-permute-start | bytes 1179656 | tf_op jit(solution)/shard_map/ppermute | solution.py:124
  116.8 3.3 copy-start.48
  116.8 3.3 copy-start.28
  120.1 10.3 %copy-start.14 = (f32[1024,768]{1,0:T(8,128)}, f32[1024,768]{1,0:T(8,128)S(1)}, u32[]{:S(2)}) copy-start(f32[1024,768]{1,0:T(8,128)S(1)} %fusion.67) | copy-start | bytes 9437188
  120.1 11.5 %copy-start.65 = (bf16[768,768]{1,0:T(8,128)(2,1)S(1)}, bf16[768,768]{1,0:T(8,128)(2,1)}, u32[]{:S(2)}) copy-start(bf16[768,768]{1,0:T(8,128)(2,1)} %param.33) | copy-start | bytes 3538948
  134.2 58.6 %reduce-scatter.7.cloned.1.call-start = ((), (), s32[]{:S(2)}) async-start(), calls=%async_computation.7 | async-start | bytes 1966080 | tf_op jit(solution)/shard_map/reduce_scatter | solution.py:105
  138.7 23.7 %copy-start.6 = (bf16[256,768]{1,0:T(8,128)(2,1)S(1)}, bf16[256,768]{1,0:T(8,128)(2,1)}, u32[]{:S(2)}) copy-start(bf16[256,768]{1,0:T(8,128)(2,1)} %reduce-scatter.5.cloned.1.call-done) | copy-start | bytes 1179652
  141.3 54.2 %copy-start.12 = (bf16[256,768]{1,0:T(8,128)(2,1)S(1)}, bf16[256,768]{1,0:T(8,128)(2,1)}, u32[]{:S(2)}) copy-start(bf16[256,768]{1,0:T(8,128)(2,1)} %param.37) | copy-start | bytes 1179652
  141.3 76.3 %all-gather.8.cloned.1.call-start = ((), (), s32[]{:S(2)}) async-start(), calls=%async_computation.9 | async-start | bytes 1966080 | tf_op jit(solution)/shard_map/all_gather | solution.py:155
  195.4 24.3 %copy-start.24 = (bf16[1024,192]{0,1:T(8,128)(2,1)S(1)}, bf16[1024,192]{0,1:T(8,128)(2,1)}, u32[]{:S(2)}) copy-start(bf16[1024,192]{0,1:T(8,128)(2,1)} %copy-done.23) | copy-start | bytes 1179652
  197.8 78.5 %reduce-scatter.11.cloned.1.call-start = ((), (), s32[]{:S(2)}) async-start(), calls=%async_computation.10 | async-start | bytes 1966080 | tf_op jit(solution)/shard_map/reduce_scatter | solution.py:207
  219.7 4.0 slice-start
  219.7 4.7 slice-start.1
  223.7 3.9 slice-start.2
  224.5 3.2 slice-start.3
  240.0 267.4 %all-reduce.5.cloned.1.call-start = ((), (), s32[]{:S(2)}) async-start(), calls=%async_computation.11 | async-start | bytes 14155776 | tf_op jit(solution)/shard_map/psum | solution.py:229
  240.3 4.9 copy-start.64
  240.4 4.9 copy-start.67
  253.3 23.0 %copy-start.41 = (f32[768]{0:T(1024)S(1)}, f32[768]{0:T(1024)}, u32[]{:S(2)}) copy-start(f32[768]{0:T(1024)} %copy-done.40) | copy-start | bytes 9220
  253.3 23.0 %copy-start.44 = (f32[256]{0:T(256)S(1)}, f32[256]{0:T(256)}, u32[]{:S(2)}) copy-start(f32[256]{0:T(256)} %copy-done.43) | copy-start | bytes 3076
  253.3 24.3 %copy-start.59 = (f32[256]{0:T(256)S(1)}, f32[256]{0:T(256)}, u32[]{:S(2)}) copy-start(f32[256]{0:T(256)} %copy-done.58) | copy-start | bytes 3076
  253.3 24.4 %copy-start.50 = (f32[256]{0:T(256)S(1)}, f32[256]{0:T(256)}, u32[]{:S(2)}) copy-start(f32[256]{0:T(256)} %copy-done.49) | copy-start | bytes 3076
  253.4 25.8 %copy-start.51 = (f32[768]{0:T(1024)S(1)}, f32[768]{0:T(1024)}, u32[]{:S(2)}) copy-start(f32[768]{0:T(1024)} %get-tuple-element.17) | copy-start | bytes 9220
  253.4 25.8 %copy-start.52 = (f32[768]{0:T(1024)S(1)}, f32[768]{0:T(1024)}, u32[]{:S(2)}) copy-start(f32[768]{0:T(1024)} %get-tuple-element.23) | copy-start | bytes 9220
  253.4 25.8 %copy-start.53 = (f32[768]{0:T(1024)S(1)}, f32[768]{0:T(1024)}, u32[]{:S(2)}) copy-start(f32[768]{0:T(1024)} %get-tuple-element.21) | copy-start | bytes 9220
  253.4 25.8 %copy-start.54 = (f32[768]{0:T(1024)S(1)}, f32[768]{0:T(1024)}, u32[]{:S(2)}) copy-start(f32[768]{0:T(1024)} %get-tuple-element.22) | copy-start | bytes 9220
  253.4 67.6 %copy-start.13 = (bf16[256,768]{1,0:T(8,128)(2,1)S(1)}, bf16[256,768]{1,0:T(8,128)(2,1)}, u32[]{:S(2)}) copy-start(bf16[256,768]{1,0:T(8,128)(2,1)} %param.37) | copy-start | bytes 1179652
  253.4 67.5 %copy-start.57 = (f32[256]{0:T(256)S(1)}, f32[256]{0:T(256)}, u32[]{:S(2)}) copy-start(f32[256]{0:T(256)} %copy-done.56) | copy-start | bytes 3076
  507.5 5.9 %copy-start.33 = (f32[192,768]{1,0:T(8,128)S(1)}, f32[192,768]{1,0:T(8,128)}, u32[]{:S(2)}) copy-start(f32[192,768]{1,0:T(8,128)} %get-tuple-element.79) | copy-start | bytes 1769476
  507.5 6.7 %copy-start.16 = (f32[768,768]{1,0:T(8,128)S(1)}, f32[768,768]{1,0:T(8,128)}, u32[]{:S(2)}) copy-start(f32[768,768]{1,0:T(8,128)} %get-tuple-element.83) | copy-start | bytes 7077892
  (35 other events, 60.9 us)
Sparse Core Ops, SparseCore 0:
  13.8 22.3 all-gather.3
  53.9 27.9 reduce-scatter.4
  87.9 25.2 all-gather.5
  134.3 28.0 reduce-scatter.8
  164.8 27.9 reduce-scatter.6
  197.9 19.6 all-gather.7
  240.2 28.0 reduce-scatter.10
  274.4 232.9 all-reduce.4
